TPU v7x, 512 devices: a whole 4x4x16 slice. The times are simulated.
512 devices in a mesh: lat: 16 (over z_hi, y), lon: 32 (over z_lo, x, core).
Axes of the slice: x: 4, y: 4, z: 16 (z_hi: 4, z_lo: 4; z = z_hi * 4 + z_lo), core: 2. Of those that a mesh axis runs over, the one named last changes fastest.
Arguments:
- queries: float32 [64, 1024, 512], P('lat', 'lon'), may hold values from -80 to 80
- key_rows: float32 [512, 512], P(('lat', 'lon')), may hold values from -8 to 8
- value_rows: float32 [512, 512], P(('lat', 'lon')), may hold values from -6 to 6
- cotangent: float32 [64, 1024, 512], P('lat', 'lon'), may hold values from -25 to 25
- conv_taps: float32 [9, 512], replicated, may hold values from -1.75 to 1.75
Outputs:
- query_grad: float32 [64, 1024, 512], P('lat', 'lon')
- key_grad: float32 [512, 512], P(('lat', 'lon'))
- value_grad: float32 [512, 512], P(('lat', 'lon'))
- tap_update: float32 [9, 512], replicated
All inputs are finite; a program needn't handle non-finite values.
Results may differ from a plain program's by a relative error of at most 0.0003.
Values sent between devices are 32-bit elements; how exact they have to be, the bound alone decides.
A program may use at most 64 MiB of HBM per device.

v0:
```python
import jax
import jax.numpy as jnp
from jax import lax
from jax.sharding import PartitionSpec as P

HD = 64
HIGH = lax.Precision.HIGHEST
OFFSETS = ((-1, -1), (-1, 0), (-1, 1), (0, -1), (0, 0), (0, 1), (1, -1), (1, 0), (1, 1))


def joined_along(pieces, dim):
    lengths = list(pieces.shape[1:])
    lengths[dim] *= pieces.shape[0]
    return jnp.moveaxis(pieces, 0, dim).reshape(lengths)


def copy_for_each(value, axis):
    copies = jnp.broadcast_to(value, (lax.axis_size(axis), *value.shape))
    return lax.all_to_all(copies, axis, split_axis=0, concat_axis=0, tiled=True)


def gather_directly(value, axis, dim):
    return joined_along(copy_for_each(value, axis), dim)


def extended(value, sides, width):
    for axis, dim in sides:
        peers, length = (lax.axis_size(axis), value.shape[dim])
        up = [(i, (i + 1) % peers) for i in range(peers)]
        down = [(j, i) for i, j in up]
        last = lax.slice_in_dim(value, length - width, length, axis=dim)
        initial = lax.slice_in_dim(value, 0, width, axis=dim)
        before = lax.ppermute(last, axis, up)
        after = lax.ppermute(initial, axis, down)
        value = jnp.concatenate([before, value, after], axis=dim)
    return value


def cut_along(value, dim, peers):
    lengths = value.shape
    pieces = value.reshape(*lengths[:dim], peers, lengths[dim] // peers, *lengths[dim + 1 :])
    return jnp.moveaxis(pieces, dim, 0)


def summed_on_arrival(value, axis, dim):
    peers = lax.axis_size(axis)
    pieces = lax.all_to_all(cut_along(value, dim, peers), axis, 0, 0, tiled=True)
    return jnp.sum(pieces, axis=0)


def split_heads(matrix):
    return matrix.reshape(matrix.shape[0], -1, HD)


def latitude_weights(row_count, band_index, band_count):
    line_total = row_count * band_count
    centres = (jnp.arange(line_total, dtype=jnp.float32) + 0.5) * (jnp.pi / line_total)
    mean_cosine = jnp.sum(jnp.sin(centres)) / line_total
    mine = (band_index * row_count + jnp.arange(row_count, dtype=jnp.int32)).astype(jnp.float32)
    return jnp.sin((mine + 0.5) * (jnp.pi / line_total)) / mean_cosine


def close_poles(padded, row_dim, band_index, band_count):
    height = padded.shape[row_dim]
    positions = jnp.arange(height)
    outside = (positions == 0) & (band_index == 0) | (positions == height - 1) & (
        band_index == band_count - 1
    )
    shape_mask = [1] * padded.ndim
    shape_mask[row_dim] = height
    return jnp.where(outside.reshape(shape_mask), 0.0, padded)


def spread_taps(weighted, grad_padded, conv_taps):
    row_count, col_count = (weighted.shape[0], weighted.shape[1])
    result = weighted
    for tap_index, (shift_row, shift_col) in enumerate(OFFSETS):
        result = (
            result
            + conv_taps[tap_index]
            * grad_padded[
                1 - shift_row : 1 - shift_row + row_count, 1 - shift_col : 1 - shift_col + col_count
            ]
        )
    return result


def tap_terms(weighted, out_padded):
    row_count, col_count = (weighted.shape[0], weighted.shape[1])
    term_list = []
    for shift_row, shift_col in OFFSETS:
        term_list.append(
            jnp.sum(
                out_padded[
                    1 + shift_row : 1 + shift_row + row_count,
                    1 + shift_col : 1 + shift_col + col_count,
                ]
                * weighted,
                axis=(0, 1),
            )
        )
    return jnp.stack(term_list)


def group_logits(query_part, key_part):
    return jnp.einsum(
        "qhd,khd->hqk", split_heads(query_part), split_heads(key_part), precision=HIGH
    ) * HD ** (-0.5)


def body(queries, key_rows, value_rows, cotangent, conv_taps):
    row_count, col_count, channels = queries.shape
    band_count = lax.axis_size("lat")
    band_index = lax.axis_index("lat")
    weighted = cotangent * latitude_weights(row_count, band_index, band_count)[:, None, None]
    paired_rows = jnp.concatenate([key_rows, value_rows], 1)
    paired_sector = gather_directly(paired_rows, "lon", 0)
    paired_all = lax.all_gather(paired_sector, "lat", axis=0, tiled=True)
    key_all = paired_all[:, :channels]
    value_all = paired_all[:, channels:]
    token_count = row_count * col_count
    key_count = key_all.shape[0]
    query_flat = queries.reshape(token_count, channels)
    group_width = 2 * HD
    group_count = channels // group_width
    outputs = []
    peaks = []
    sums_soft = []
    for group_index in range(group_count):
        col_start = group_index * group_width
        col_stop = col_start + group_width
        logits = group_logits(query_flat[:, col_start:col_stop], key_all[:, col_start:col_stop])
        row_peak = jnp.max(logits, -1, keepdims=True)
        raised = jnp.exp(logits - row_peak)
        normaliser = jnp.sum(raised, -1, keepdims=True)
        soft_weights = raised / normaliser
        outputs.append(
            jnp.einsum(
                "hqk,khd->qhd",
                soft_weights,
                split_heads(value_all[:, col_start:col_stop]),
                precision=HIGH,
            ).reshape(token_count, group_width)
        )
        peaks.append(row_peak)
        sums_soft.append(normaliser)
    out_flat = jnp.concatenate(outputs, 1)
    out_grid = out_flat.reshape(row_count, col_count, channels)
    both_padded = close_poles(
        extended(jnp.stack([weighted, out_grid]), (("lat", 1), ("lon", 2)), 1),
        1,
        band_index,
        band_count,
    )
    grad_padded = both_padded[0]
    out_padded = both_padded[1]
    out_grad = spread_taps(weighted, grad_padded, conv_taps)
    tap_sum = lax.psum(tap_terms(weighted, out_padded), ("lat", "lon"))
    tap_update = tap_sum / jnp.sqrt(jnp.mean(tap_sum * tap_sum) + 1e-06)
    grad_flat = out_grad.reshape(token_count, channels)
    query_parts = []
    key_parts = []
    value_parts = []
    for group_index in range(group_count):
        col_start = group_index * group_width
        col_stop = col_start + group_width
        query_heads = split_heads(query_flat[:, col_start:col_stop])
        key_heads = split_heads(key_all[:, col_start:col_stop])
        logits = jnp.einsum("qhd,khd->hqk", query_heads, key_heads, precision=HIGH) * HD ** (-0.5)
        soft_weights = jnp.exp(logits - peaks[group_index]) / sums_soft[group_index]
        grad_heads = split_heads(grad_flat[:, col_start:col_stop])
        value_parts.append(
            jnp.einsum("hqk,qhd->khd", soft_weights, grad_heads, precision=HIGH).reshape(
                key_count, group_width
            )
        )
        prob_grad = jnp.einsum(
            "qhd,khd->hqk",
            grad_heads,
            split_heads(value_all[:, col_start:col_stop]),
            precision=HIGH,
        )
        row_dot = jnp.transpose(
            jnp.sum(grad_heads * split_heads(out_flat[:, col_start:col_stop]), -1)
        )[:, :, None]
        logit_grad = soft_weights * (prob_grad - row_dot)
        query_parts.append(
            (
                jnp.einsum("hqk,khd->qhd", logit_grad, key_heads, precision=HIGH) * HD ** (-0.5)
            ).reshape(token_count, group_width)
        )
        key_parts.append(
            (
                jnp.einsum("hqk,qhd->khd", logit_grad, query_heads, precision=HIGH) * HD ** (-0.5)
            ).reshape(key_count, group_width)
        )
    paired_terms = jnp.concatenate(key_parts + value_parts, 1)
    paired_band = lax.psum_scatter(paired_terms, "lat", scatter_dimension=0, tiled=True)
    paired_grad = summed_on_arrival(paired_band, "lon", 0)
    key_grad = paired_grad[:, :channels]
    value_grad = paired_grad[:, channels:]
    query_grad = jnp.concatenate(query_parts, 1).reshape(row_count, col_count, channels)
    return (query_grad, key_grad, value_grad, tap_update)


def solution(mesh):
    placed = (
        P("lat", "lon", None),
        P(("lat", "lon"), None),
        P(("lat", "lon"), None),
        P("lat", "lon", None),
        P(),
    )
    return jax.shard_map(
        body,
        mesh=mesh,
        in_specs=placed,
        out_specs=(P("lat", "lon", None), P(("lat", "lon"), None), P(("lat", "lon"), None), P()),
        check_vma=False,
    )
```

profile of v0, /device:TPU:1, one launch (start us, length us, event | category | flops | bytes accessed | tf_op | source)
XLA Modules:
  0.0 343.2 jit_solution(12765066276765064027)
XLA Ops:
  8.0 18.8 %all_to_all.10 = f32[32,1,1024]{2,1,0:T(1,128)} all-to-all(f32[32,1,1024]{2,1,0:T(1,128)S(1)} %broadcast_in_dim.10), channel_id=1, replica_groups=mesh['lat'=16,'lon'=32] {'lon'}, dimensions={0} | all-to-all | bytes 262144 | tf_op jit(solution)/shard_map/all_to_all | solution.py:19
  26.9 1.0 fusion.53
  30.8 1.0 fusion.50
  31.8 88.1 %all-gather.3.cloned.1.call-done = f32[512,1,1024]{2,1,0:T(1,128)} async-done(((f32[32,1,1024]{2,1,0:T(1,128)}), f32[512,1,1024]{2,1,0:T(1,128)}) %all-gather.3.cloned.1.call-update) | async-done | bytes 2097168 | tf_op jit(solution)/shard_map/all_gather | solution.py:118
  120.0 2.1 copy.158
  124.8 1.0 fusion.56
  126.7 1.0 fusion.58
  127.8 1.1 convolution_bitcast_fusion.2
  130.0 1.0 fusion.57
  131.9 1.0 fusion.59
  133.1 1.4 convolution_bitcast_fusion.3
  134.8 2.1 collective-permute-start
  136.9 9.2 %collective-permute-start.1 = (f32[2,1,32,512]{3,2,1,0:T(8,128)S(1)}, f32[2,1,32,512]{3,2,1,0:T(8,128)S(1)}, u32[]{:S(2)}, u32[]{:S(2)}) collective-permute-start(f32[2,1,32,512]{3,2,1,0:T(8,128)S(1)} %get-tuple-element.26), channel_id=1, source_target_pairs={{32,0},{64,32},{96,64},{128,96},{160,128},{192,160},{224,192},{256... | collective-permute-start | bytes 393224 | tf_op jit(solution)/shard_map/ppermute | solution.py:34
  146.1 4.7 %collective-permute-done = f32[2,1,32,512]{3,2,1,0:T(8,128)S(1)} collective-permute-done((f32[2,1,32,512]{3,2,1,0:T(8,128)S(1)}, f32[2,1,32,512]{3,2,1,0:T(8,128)S(1)}, u32[]{:S(2)}, u32[]{:S(2)}) %collective-permute-start) | collective-permute-done | bytes 131104 | tf_op jit(solution)/shard_map/ppermute | solution.py:33
  150.9 3.2 collective-permute-start.2
  154.1 2.1 collective-permute-start.3
  156.3 3.3 collective-permute-done.3
  160.9 1.6 copy.153
  163.3 1.6 copy.155
  165.8 1.6 copy.154
  168.2 1.6 copy.156
  170.8 1.6 fusion.38
  172.4 1.0 fusion
  174.9 1.0 fusion.2
  177.4 1.0 fusion.1
  179.9 1.0 fusion.3
  181.8 1.9 copy.146
  184.1 117.4 %psum.7 = f32[9,512]{1,0:T(8,128)S(1)} all-reduce(f32[9,512]{1,0:T(8,128)S(1)} %stack.47), channel_id=1, replica_groups=mesh['lat'=16,'lon'=32] {'lat','lon'}, use_global_device_ids=true, to_apply=%region_24.25 | all-reduce | flops 4608 | bytes 36864 | tf_op jit(solution)/shard_map/psum | solution.py:158
  304.9 13.6 %reduce-scatter.4.cloned.1.call-done = f32[32,1024]{1,0:T(8,128)} async-done(((f32[512,1024]{1,0:T(8,128)}), f32[32,1024]{1,0:T(8,128)}) %reduce-scatter.4.cloned.1.call-update) | async-done | bytes 131088
  318.5 1.1 copy.147
  320.4 6.7 %all-to-all-start.1 = ((f32[32,1,1024]{2,1,0:T(1,128)}), f32[32,1,1024]{2,1,0:T(1,128)S(1)}, u32[]{:S(2)}, u32[]{:S(2)}) async-start(f32[32,1,1024]{2,1,0:T(1,128)} %copy.125), calls=%async_computation.1 | async-start | bytes 262144 | tf_op jit(solution)/shard_map/all_to_all | solution.py:47
  329.2 6.5 %all-to-all-done.1 = f32[32,1,1024]{2,1,0:T(1,128)S(1)} async-done(((f32[32,1,1024]{2,1,0:T(1,128)}), f32[32,1,1024]{2,1,0:T(1,128)S(1)}, u32[]{:S(2)}, u32[]{:S(2)}) %all-to-all-start.1) | async-done | bytes 131104 | tf_op jit(solution)/shard_map/all_to_all | solution.py:47
  (154 shorter events, 25.7 us)
Async XLA Ops:
  7.2 112.8 %all-gather.3.cloned.1.call-start = ((), (), s32[]{:S(2)}) async-start(), calls=%async_computation.3 | async-start | bytes 2228224 | tf_op jit(solution)/shard_map/all_gather | solution.py:118
  26.8 291.7 %reduce-scatter.4.cloned.1.call-start = ((), (), s32[]{:S(2)}) async-start(), calls=%async_computation.4 | async-start | bytes 2228224
  29.4 95.3 %copy-start.17 = (f32[128,128]{0,1:T(8,128)}, f32[128,128]{0,1:T(8,128)S(1)}, u32[]{:S(2)}) copy-start(f32[128,128]{0,1:T(8,128)S(1)} %copy.152) | copy-start | bytes 196612
  122.5 3.4 copy-start.1
  122.6 3.8 %copy-start.28 = (f32[512,128]{0,1:T(8,128)}, f32[512,128]{0,1:T(8,128)S(1)}, u32[]{:S(2)}) copy-start(f32[512,128]{0,1:T(8,128)S(1)} %copy.96) | copy-start | bytes 786436
  123.8 2.9 copy-start.3
  123.9 3.9 %copy-start.26 = (f32[512,128]{0,1:T(8,128)}, f32[512,128]{0,1:T(8,128)S(1)}, u32[]{:S(2)}) copy-start(f32[512,128]{0,1:T(8,128)S(1)} %copy.86) | copy-start | bytes 786436
  123.9 2.8 copy-start.15
  126.4 3.6 %copy-start.19 = (f32[128,2,64]{0,2,1:T(8,128)}, f32[128,2,64]{0,2,1:T(8,128)S(1)}, u32[]{:S(2)}) copy-start(f32[128,2,64]{0,2,1:T(8,128)S(1)} %convolution_bitcast_fusion) | copy-start | bytes 196612
  126.4 3.6 %copy-start.13 = (f32[128,128]{0,1:T(8,128)S(1)}, f32[128,128]{0,1:T(8,128)}, u32[]{:S(2)}) copy-start(f32[128,128]{0,1:T(8,128)} %copy.151) | copy-start | bytes 196612
  127.7 3.4 %copy-start.24 = (f32[512,128]{0,1:T(8,128)S(1)}, f32[512,128]{0,1:T(8,128)}, u32[]{:S(2)}) copy-start(f32[512,128]{0,1:T(8,128)} %copy.91) | copy-start | bytes 786436
  131.7 19.2 %copy-start.21 = (f32[128,2,64]{0,2,1:T(8,128)}, f32[128,2,64]{0,2,1:T(8,128)S(1)}, u32[]{:S(2)}) copy-start(f32[128,2,64]{0,2,1:T(8,128)S(1)} %convolution_bitcast_fusion.1) | copy-start | bytes 196612
  132.9 13.2 %copy-start.34 = (f32[9,512]{1,0:T(8,128)S(1)}, f32[9,512]{1,0:T(8,128)}, u32[]{:S(2)}) copy-start(f32[9,512]{1,0:T(8,128)} %param.9) | copy-start | bytes 55300
  134.5 16.3 %copy-start.22 = (f32[128,2,64]{0,2,1:T(8,128)}, f32[128,2,64]{0,2,1:T(8,128)S(1)}, u32[]{:S(2)}) copy-start(f32[128,2,64]{0,2,1:T(8,128)S(1)} %convolution_bitcast_fusion.3) | copy-start | bytes 196612
  134.8 16.0 %collective-permute-start = (f32[2,1,32,512]{3,2,1,0:T(8,128)S(1)}, f32[2,1,32,512]{3,2,1,0:T(8,128)S(1)}, u32[]{:S(2)}, u32[]{:S(2)}) collective-permute-start(f32[2,1,32,512]{3,2,1,0:T(8,128)S(1)} %get-tuple-element.25), channel_id=1, source_target_pairs={{0,32},{32,64},{64,96},{96,128},{128,160},{160,192},{192,224},{224... | collective-permute-start | bytes 393224 | tf_op jit(solution)/shard_map/ppermute | solution.py:33
  136.9 13.9 %collective-permute-start.1 = (f32[2,1,32,512]{3,2,1,0:T(8,128)S(1)}, f32[2,1,32,512]{3,2,1,0:T(8,128)S(1)}, u32[]{:S(2)}, u32[]{:S(2)}) collective-permute-start(f32[2,1,32,512]{3,2,1,0:T(8,128)S(1)} %get-tuple-element.26), channel_id=1, source_target_pairs={{32,0},{64,32},{96,64},{128,96},{160,128},{192,160},{224,192},{256... | collective-permute-start | bytes 393224 | tf_op jit(solution)/shard_map/ppermute | solution.py:34
  150.9 9.0 %copy-start = (f32[4,32,512]{2,1,0:T(8,128)S(1)}, f32[4,32,512]{2,1,0:T(8,128)}, u32[]{:S(2)}) copy-start(f32[4,32,512]{2,1,0:T(8,128)} %param.8) | copy-start | bytes 786436
  150.9 5.4 %collective-permute-start.2 = (f32[2,6,1,512]{3,2,1,0:T(1,128)S(1)}, f32[2,6,1,512]{3,2,1,0:T(1,128)S(1)}, u32[]{:S(2)}, u32[]{:S(2)}) collective-permute-start(f32[2,6,1,512]{3,2,1,0:T(1,128)S(1)} %get-tuple-element.23), channel_id=1, source_target_pairs={{0,1},{1,2},{2,3},{3,4},{4,5},{5,6},{6,7},{7,8},{8,9},{9,10},{10,1... | collective-permute-start | bytes 73736 | tf_op jit(solution)/shard_map/ppermute | solution.py:33
  154.1 5.4 %collective-permute-start.3 = (f32[2,6,1,512]{3,2,1,0:T(1,128)S(1)}, f32[2,6,1,512]{3,2,1,0:T(1,128)S(1)}, u32[]{:S(2)}, u32[]{:S(2)}) collective-permute-start(f32[2,6,1,512]{3,2,1,0:T(1,128)S(1)} %get-tuple-element.24), channel_id=1, source_target_pairs={{1,0},{2,1},{3,2},{4,3},{5,4},{6,5},{7,6},{8,7},{9,8},{10,9},{11,1... | collective-permute-start | bytes 73736 | tf_op jit(solution)/shard_map/ppermute | solution.py:34
  159.9 9.9 %copy-start.20 = (f32[128,2,64]{0,2,1:T(8,128)S(1)}, f32[128,2,64]{0,2,1:T(8,128)}, u32[]{:S(2)}) copy-start(f32[128,2,64]{0,2,1:T(8,128)} %copy-done.19) | copy-start | bytes 196612
  169.8 2.5 copy-start.29
  169.8 2.5 copy-start.33
  170.7 2.6 copy-start.18
  170.7 3.4 copy-start.32
  174.8 2.5 copy-start.25
  183.7 119.1 %copy-start.2 = (f32[512,128]{0,1:T(8,128)S(1)}, f32[512,128]{0,1:T(8,128)}, u32[]{:S(2)}) copy-start(f32[512,128]{0,1:T(8,128)} %copy-done.1) | copy-start | bytes 786436
  183.7 119.1 %copy-start.8 = (f32[2,128,512]{1,2,0:T(8,128)S(1)}, f32[2,128,512]{1,2,0:T(8,128)}, u32[]{:S(2)}) copy-start(f32[2,128,512]{1,2,0:T(8,128)} %copy-done.7) | copy-start | bytes 1572868
  183.7 119.8 %copy-start.4 = (f32[512,128]{0,1:T(8,128)S(1)}, f32[512,128]{0,1:T(8,128)}, u32[]{:S(2)}) copy-start(f32[512,128]{0,1:T(8,128)} %copy-done.3) | copy-start | bytes 786436
  183.7 119.8 %copy-start.10 = (f32[2,128,512]{1,2,0:T(8,128)S(1)}, f32[2,128,512]{1,2,0:T(8,128)}, u32[]{:S(2)}) copy-start(f32[2,128,512]{1,2,0:T(8,128)} %copy-done.9) | copy-start | bytes 1572868
  183.7 120.5 %copy-start.12 = (f32[2,128,512]{1,2,0:T(8,128)S(1)}, f32[2,128,512]{1,2,0:T(8,128)}, u32[]{:S(2)}) copy-start(f32[2,128,512]{1,2,0:T(8,128)} %copy-done.11) | copy-start | bytes 1572868
  303.4 23.7 %copy-start.6 = (f32[2,128,512]{1,2,0:T(8,128)S(1)}, f32[2,128,512]{1,2,0:T(8,128)}, u32[]{:S(2)}) copy-start(f32[2,128,512]{1,2,0:T(8,128)} %copy-done.5) | copy-start | bytes 1572868
  320.4 15.2 %all-to-all-start.1 = ((f32[32,1,1024]{2,1,0:T(1,128)}), f32[32,1,1024]{2,1,0:T(1,128)S(1)}, u32[]{:S(2)}, u32[]{:S(2)}) async-start(f32[32,1,1024]{2,1,0:T(1,128)} %copy.125), calls=%async_computation.1 | async-start | bytes 262144 | tf_op jit(solution)/shard_map/all_to_all | solution.py:47
  (10 other events, 20.8 us)
Sparse Core Ops, SparseCore 0:
  26.9 93.0 all-gather.2
  183.8 134.6 reduce-scatter.3
where the time goes:
time: 344 us; the launch traced here: 343 us
  blocking collectives  136 us (40%)
  waiting for transfers between devices  116 us (34%)
  starting transfers between devices  23.4 us (7%)
  local copies, waits for them, and re-layouts  21.9 us (6%)
  matrix products  19.9 us (6%)
  between operations  16.2 us (5%)
  other arithmetic  9.35 us (3%)
    psum x1, blocking collectives, body(): tap_sum = lax.psum(tap_terms(weighted, out_padded), ('lat', 'lon'))  117 us
    all_gather x1, waiting for transfers between devices, body(): paired_all = lax.all_gather(paired_sector, 'lat', axis=0, tiled=True)  88.1 us
    all_to_all x1, blocking collectives, copy_for_each(): return lax.all_to_all(copies, axis, split_axis=0, concat_axis=0, tiled=True)  18.8 us
    unnamed x3, waiting for transfers between devices  13.6 us
    unnamed x88, local copies, waits for them, and re-layouts  13.2 us
    ppermute x2, starting transfers between devices, extended(): after = lax.ppermute(initial, axis, down)  11.3 us
  transfers between devices with their start and end apart: 7, of which 5 were waited for; matrix products, arithmetic and copies ran while one was open for 3% of the time, Pallas kernels for 0%

commit v1 on v0

--- a/solution.py
+++ b/solution.py
@@ -155,7 +155,7 @@
     grad_padded = both_padded[0]
     out_padded = both_padded[1]
     out_grad = spread_taps(weighted, grad_padded, conv_taps)
-    tap_sum = lax.psum(tap_terms(weighted, out_padded), ("lat", "lon"))
+    tap_sum = lax.psum(lax.psum(tap_terms(weighted, out_padded), "lon"), "lat")
     tap_update = tap_sum / jnp.sqrt(jnp.mean(tap_sum * tap_sum) + 1e-06)
     grad_flat = out_grad.reshape(token_count, channels)
     query_parts = []

time: 344 us -> 454 us (1.32)
  blocking collectives: 136 us -> 243 us
  starting transfers between devices: 23.4 us -> 40.2 us
  waiting for transfers between devices: 116 us -> 103 us
    psum x1 -> x2, blocking collectives: 117 us -> 224 us  [body(): tap_sum = lax.psum(lax.psum(tap_terms(weighted, out_padded), 'lon'), 'lat')]
    all_to_all x1, starting transfers between devices: 6.68 us -> 23.5 us  [summed_on_arrival(): lax.all_to_all(cut_along(value, dim, peers), axis, 0, 0, tiled=True)]
    unnamed x3, waiting for transfers between devices: 13.6 us -> 0.04 us
  transfers between devices with their start and end apart: 7 -> 7, of which waited for: 5 -> 4; matrix products, arithmetic and copies ran while one was open for 3% -> 2% of each run, Pallas kernels for 0% -> 0%
where the time goes in v1:
time: 454 us; the launch traced here: 453 us
  blocking collectives  243 us (54%)
  waiting for transfers between devices  103 us (23%)
  starting transfers between devices  40.2 us (9%)
  local copies, waits for them, and re-layouts  21.9 us (5%)
  matrix products  19.9 us (4%)
  between operations  16.2 us (4%)
  other arithmetic  9.35 us (2%)
    psum x2, blocking collectives, body(): tap_sum = lax.psum(lax.psum(tap_terms(weighted, out_padded), 'lon'), 'lat')  224 us
    all_gather x1, waiting for transfers between devices, body(): paired_all = lax.all_gather(paired_sector, 'lat', axis=0, tiled=True)  88.1 us
    all_to_all x1, starting transfers between devices, summed_on_arrival(): lax.all_to_all(cut_along(value, dim, peers), axis, 0, 0, tiled=True)  23.5 us
    all_to_all x1, blocking collectives, copy_for_each(): return lax.all_to_all(copies, axis, split_axis=0, concat_axis=0, tiled=True)  18.8 us
    unnamed x88, local copies, waits for them, and re-layouts  13.2 us
    ppermute x2, starting transfers between devices, extended(): after = lax.ppermute(initial, axis, down)  11.3 us
  transfers between devices with their start and end apart: 7, of which 4 were waited for; matrix products, arithmetic and copies ran while one was open for 2% of the time, Pallas kernels for 0%

profile of v1, /device:TPU:1, one launch (start us, length us, event | category | flops | bytes accessed | tf_op | source)
XLA Modules:
  0.0 453.0 jit_solution(11724858027187844671)
XLA Ops:
  8.0 18.8 %all_to_all.10 = f32[32,1,1024]{2,1,0:T(1,128)} all-to-all(f32[32,1,1024]{2,1,0:T(1,128)S(1)} %broadcast_in_dim.10), channel_id=1, replica_groups=mesh['lat'=16,'lon'=32] {'lon'}, dimensions={0} | all-to-all | bytes 262144 | tf_op jit(solution)/shard_map/all_to_all | solution.py:19
  26.9 1.0 fusion.53
  30.8 1.0 fusion.50
  31.8 88.1 %all-gather.3.cloned.1.call-done = f32[512,1,1024]{2,1,0:T(1,128)} async-done(((f32[32,1,1024]{2,1,0:T(1,128)}), f32[512,1,1024]{2,1,0:T(1,128)}) %all-gather.3.cloned.1.call-update) | async-done | bytes 2097168 | tf_op jit(solution)/shard_map/all_gather | solution.py:118
  120.0 2.1 copy.158
  124.8 1.0 fusion.56
  126.7 1.0 fusion.58
  127.8 1.1 convolution_bitcast_fusion.2
  130.0 1.0 fusion.57
  131.9 1.0 fusion.59
  133.1 1.4 convolution_bitcast_fusion.3
  134.8 2.1 collective-permute-start
  136.9 9.2 %collective-permute-start.1 = (f32[2,1,32,512]{3,2,1,0:T(8,128)S(1)}, f32[2,1,32,512]{3,2,1,0:T(8,128)S(1)}, u32[]{:S(2)}, u32[]{:S(2)}) collective-permute-start(f32[2,1,32,512]{3,2,1,0:T(8,128)S(1)} %get-tuple-element.26), channel_id=1, source_target_pairs={{32,0},{64,32},{96,64},{128,96},{160,128},{192,160},{224,192},{256... | collective-permute-start | bytes 393224 | tf_op jit(solution)/shard_map/ppermute | solution.py:34
  146.1 4.7 %collective-permute-done = f32[2,1,32,512]{3,2,1,0:T(8,128)S(1)} collective-permute-done((f32[2,1,32,512]{3,2,1,0:T(8,128)S(1)}, f32[2,1,32,512]{3,2,1,0:T(8,128)S(1)}, u32[]{:S(2)}, u32[]{:S(2)}) %collective-permute-start) | collective-permute-done | bytes 131104 | tf_op jit(solution)/shard_map/ppermute | solution.py:33
  150.9 3.2 collective-permute-start.2
  154.1 2.1 collective-permute-start.3
  156.3 3.3 collective-permute-done.3
  160.9 1.6 copy.153
  163.3 1.6 copy.155
  165.8 1.6 copy.154
  168.2 1.6 copy.156
  170.8 1.6 fusion.38
  172.4 1.0 fusion
  174.9 1.0 fusion.2
  177.4 1.0 fusion.1
  179.9 1.0 fusion.3
  181.8 1.9 copy.146
  184.1 137.3 %psum.14 = f32[9,512]{1,0:T(8,128)S(1)} all-reduce(f32[9,512]{1,0:T(8,128)S(1)} %stack.47), channel_id=1, replica_groups=mesh['lat'=16,'lon'=32] {'lon'}, use_global_device_ids=true, to_apply=%region_24.25 | all-reduce | flops 4608 | bytes 36864 | tf_op jit(solution)/shard_map/psum | solution.py:158
  321.4 86.6 %psum.15 = f32[9,512]{1,0:T(8,128)S(1)} all-reduce(f32[9,512]{1,0:T(8,128)S(1)} %psum.14), channel_id=1, replica_groups=mesh['lat'=16,'lon'=32] {'lat'}, use_global_device_ids=true, to_apply=%region_25.26 | all-reduce | flops 4608 | bytes 36864 | tf_op jit(solution)/shard_map/psum | solution.py:158
  411.5 1.1 copy.147
  413.4 23.5 %all-to-all-start.1 = ((f32[32,1,1024]{2,1,0:T(1,128)}), f32[32,1,1024]{2,1,0:T(1,128)S(1)}, u32[]{:S(2)}, u32[]{:S(2)}) async-start(f32[32,1,1024]{2,1,0:T(1,128)} %copy.125), calls=%async_computation.1 | async-start | bytes 262144 | tf_op jit(solution)/shard_map/all_to_all | solution.py:47
  438.9 6.6 %all-to-all-done.1 = f32[32,1,1024]{2,1,0:T(1,128)S(1)} async-done(((f32[32,1,1024]{2,1,0:T(1,128)}), f32[32,1,1024]{2,1,0:T(1,128)S(1)}, u32[]{:S(2)}, u32[]{:S(2)}) %all-to-all-start.1) | async-done | bytes 131104 | tf_op jit(solution)/shard_map/all_to_all | solution.py:47
  (155 shorter events, 25.7 us)
Async XLA Ops:
  7.2 112.8 %all-gather.3.cloned.1.call-start = ((), (), s32[]{:S(2)}) async-start(), calls=%async_computation.3 | async-start | bytes 2228224 | tf_op jit(solution)/shard_map/all_gather | solution.py:118
  26.8 384.6 %reduce-scatter.4.cloned.1.call-start = ((), (), s32[]{:S(2)}) async-start(), calls=%async_computation.4 | async-start | bytes 2228224
  29.4 95.3 %copy-start.17 = (f32[128,128]{0,1:T(8,128)}, f32[128,128]{0,1:T(8,128)S(1)}, u32[]{:S(2)}) copy-start(f32[128,128]{0,1:T(8,128)S(1)} %copy.152) | copy-start | bytes 196612
  122.5 3.4 copy-start.1
  122.6 3.8 copy-start.28
  123.8 2.9 copy-start.3
  123.9 3.9 copy-start.26
  123.9 2.8 copy-start.15
  126.4 3.6 copy-start.19
  126.4 3.6 copy-start.13
  127.7 3.4 copy-start.24
  131.7 19.2 %copy-start.21 = (f32[128,2,64]{0,2,1:T(8,128)}, f32[128,2,64]{0,2,1:T(8,128)S(1)}, u32[]{:S(2)}) copy-start(f32[128,2,64]{0,2,1:T(8,128)S(1)} %convolution_bitcast_fusion.1) | copy-start | bytes 196612
  132.9 13.2 %copy-start.34 = (f32[9,512]{1,0:T(8,128)S(1)}, f32[9,512]{1,0:T(8,128)}, u32[]{:S(2)}) copy-start(f32[9,512]{1,0:T(8,128)} %param.9) | copy-start | bytes 55300
  134.5 16.3 %copy-start.22 = (f32[128,2,64]{0,2,1:T(8,128)}, f32[128,2,64]{0,2,1:T(8,128)S(1)}, u32[]{:S(2)}) copy-start(f32[128,2,64]{0,2,1:T(8,128)S(1)} %convolution_bitcast_fusion.3) | copy-start | bytes 196612
  134.8 16.0 %collective-permute-start = (f32[2,1,32,512]{3,2,1,0:T(8,128)S(1)}, f32[2,1,32,512]{3,2,1,0:T(8,128)S(1)}, u32[]{:S(2)}, u32[]{:S(2)}) collective-permute-start(f32[2,1,32,512]{3,2,1,0:T(8,128)S(1)} %get-tuple-element.25), channel_id=1, source_target_pairs={{0,32},{32,64},{64,96},{96,128},{128,160},{160,192},{192,224},{224... | collective-permute-start | bytes 393224 | tf_op jit(solution)/shard_map/ppermute | solution.py:33
  136.9 13.9 %collective-permute-start.1 = (f32[2,1,32,512]{3,2,1,0:T(8,128)S(1)}, f32[2,1,32,512]{3,2,1,0:T(8,128)S(1)}, u32[]{:S(2)}, u32[]{:S(2)}) collective-permute-start(f32[2,1,32,512]{3,2,1,0:T(8,128)S(1)} %get-tuple-element.26), channel_id=1, source_target_pairs={{32,0},{64,32},{96,64},{128,96},{160,128},{192,160},{224,192},{256... | collective-permute-start | bytes 393224 | tf_op jit(solution)/shard_map/ppermute | solution.py:34
  150.9 9.0 %copy-start = (f32[4,32,512]{2,1,0:T(8,128)S(1)}, f32[4,32,512]{2,1,0:T(8,128)}, u32[]{:S(2)}) copy-start(f32[4,32,512]{2,1,0:T(8,128)} %param.8) | copy-start | bytes 786436
  150.9 5.4 %collective-permute-start.2 = (f32[2,6,1,512]{3,2,1,0:T(1,128)S(1)}, f32[2,6,1,512]{3,2,1,0:T(1,128)S(1)}, u32[]{:S(2)}, u32[]{:S(2)}) collective-permute-start(f32[2,6,1,512]{3,2,1,0:T(1,128)S(1)} %get-tuple-element.23), channel_id=1, source_target_pairs={{0,1},{1,2},{2,3},{3,4},{4,5},{5,6},{6,7},{7,8},{8,9},{9,10},{10,1... | collective-permute-start | bytes 73736 | tf_op jit(solution)/shard_map/ppermute | solution.py:33
  154.1 5.4 %collective-permute-start.3 = (f32[2,6,1,512]{3,2,1,0:T(1,128)S(1)}, f32[2,6,1,512]{3,2,1,0:T(1,128)S(1)}, u32[]{:S(2)}, u32[]{:S(2)}) collective-permute-start(f32[2,6,1,512]{3,2,1,0:T(1,128)S(1)} %get-tuple-element.24), channel_id=1, source_target_pairs={{1,0},{2,1},{3,2},{4,3},{5,4},{6,5},{7,6},{8,7},{9,8},{10,9},{11,1... | collective-permute-start | bytes 73736 | tf_op jit(solution)/shard_map/ppermute | solution.py:34
  159.9 9.9 %copy-start.20 = (f32[128,2,64]{0,2,1:T(8,128)S(1)}, f32[128,2,64]{0,2,1:T(8,128)}, u32[]{:S(2)}) copy-start(f32[128,2,64]{0,2,1:T(8,128)} %copy-done.19) | copy-start | bytes 196612
  169.8 2.5 copy-start.29
  169.8 2.5 copy-start.33
  170.7 2.6 copy-start.18
  170.7 3.4 copy-start.32
  174.8 2.5 copy-start.25
  183.7 225.6 %copy-start.2 = (f32[512,128]{0,1:T(8,128)S(1)}, f32[512,128]{0,1:T(8,128)}, u32[]{:S(2)}) copy-start(f32[512,128]{0,1:T(8,128)} %copy-done.1) | copy-start | bytes 786436
  183.7 225.7 %copy-start.8 = (f32[2,128,512]{1,2,0:T(8,128)S(1)}, f32[2,128,512]{1,2,0:T(8,128)}, u32[]{:S(2)}) copy-start(f32[2,128,512]{1,2,0:T(8,128)} %copy-done.7) | copy-start | bytes 1572868
  183.7 226.3 %copy-start.4 = (f32[512,128]{0,1:T(8,128)S(1)}, f32[512,128]{0,1:T(8,128)}, u32[]{:S(2)}) copy-start(f32[512,128]{0,1:T(8,128)} %copy-done.3) | copy-start | bytes 786436
  183.7 226.3 %copy-start.10 = (f32[2,128,512]{1,2,0:T(8,128)S(1)}, f32[2,128,512]{1,2,0:T(8,128)}, u32[]{:S(2)}) copy-start(f32[2,128,512]{1,2,0:T(8,128)} %copy-done.9) | copy-start | bytes 1572868
  183.7 227.0 %copy-start.12 = (f32[2,128,512]{1,2,0:T(8,128)S(1)}, f32[2,128,512]{1,2,0:T(8,128)}, u32[]{:S(2)}) copy-start(f32[2,128,512]{1,2,0:T(8,128)} %copy-done.11) | copy-start | bytes 1572868
  409.9 27.0 %copy-start.6 = (f32[2,128,512]{1,2,0:T(8,128)S(1)}, f32[2,128,512]{1,2,0:T(8,128)}, u32[]{:S(2)}) copy-start(f32[2,128,512]{1,2,0:T(8,128)} %copy-done.5) | copy-start | bytes 1572868
  413.4 32.1 %all-to-all-start.1 = ((f32[32,1,1024]{2,1,0:T(1,128)}), f32[32,1,1024]{2,1,0:T(1,128)S(1)}, u32[]{:S(2)}, u32[]{:S(2)}) async-start(f32[32,1,1024]{2,1,0:T(1,128)} %copy.125), calls=%async_computation.1 | async-start | bytes 262144 | tf_op jit(solution)/shard_map/all_to_all | solution.py:47
  (10 other events, 20.8 us)
Sparse Core Ops, SparseCore 0:
  26.9 93.0 all-gather.2
  183.8 132.4 reduce-scatter.3
